TPU v7x, 32 devices: a whole 2x2x4 slice. The times are simulated.
32 devices in a mesh: rep: 2 (over y), grp: 8 (over z, x), sub: 2 (over core).
Axes of the slice: x: 2, y: 2, z: 4, core: 2. Of those that a mesh axis runs over, the one named last changes fastest.
Arguments:
- query_rows: bfloat16 [16, 4, 5120], P(('grp', 'sub'), 'rep'), parts along dimension 1, may hold values from -120 to 120
- cache_keys: bfloat16 [16, 4, 128, 1024], P(('grp', 'sub'), 'rep'), parts along dimension 1, may hold values from -6 to 6
- cache_values: bfloat16 [16, 4, 128, 1024], P(('grp', 'sub'), 'rep'), parts along dimension 1, may hold values from -6 to 6
- residual: bfloat16 [16, 4, 5120], P(('grp', 'sub'), 'rep'), parts along dimension 1, may hold values from -6 to 6
- lengths: int32 [16, 4], P(('grp', 'sub'), 'rep'), parts along dimension 1, may hold values from 3 to 128
- expert_ids: int32 [16, 4, 1], P(('grp', 'sub'), 'rep'), parts along dimension 1, may hold values from 0 to 3; in each aligned block of 2 rows (0 to 1, 2 to 3, ..., all dimensions but the last counted through in order) at most 2 rows name the same one
- capacity: int32 [4], replicated, may hold values from 1 to 2
- norm_gain: float32 [5120], replicated, may hold values from 0.5 to 1.5
- router: bfloat16 [5120, 4], replicated, may hold values from -0.078125 to 0.078125
- shared_gate: bfloat16 [5120, 8192], P(None, ('grp', 'sub')), may hold values from -0.078125 to 0.078125
- shared_up: bfloat16 [5120, 8192], P(None, ('grp', 'sub')), may hold values from -0.078125 to 0.078125
- shared_down: bfloat16 [8192, 5120], P(('grp', 'sub')), may hold values from -0.0625 to 0.0625
- expert_gate: bfloat16 [5120, 32768], P(None, ('grp', 'sub')), may hold values from -0.078125 to 0.078125
- expert_up: bfloat16 [5120, 32768], P(None, ('grp', 'sub')), may hold values from -0.078125 to 0.078125
- expert_down: bfloat16 [32768, 5120], P(('grp', 'sub')), may hold values from -0.0625 to 0.0625
Outputs:
- layer_out: bfloat16 [16, 4, 5120], P(('grp', 'sub'), 'rep'), parts along dimension 1
There are 2 independent parts, one for each index of `rep`. A program takes and returns all parts, laid end to end along the dimension named above; an argument that names none is the same for every part. Nothing has to cross between parts.
Inputs may be any that keep to these rules, and one draw needn't show every extreme that they name: `expert_ids`: in each aligned block of 2 rows (the rows of one device), no expert is named more than 2 times.
All inputs are finite; a program needn't handle non-finite values.
Results may differ from a plain program's by a relative error of at most 0.0075.
Values may be sent and summed in bfloat16 or wider, within the bound.
No kernel may reach another device: no remote copies, remote signals or barrier semaphores. Data moves between devices by JAX's collectives and lax.ppermute only.
A program may use at most 128 MiB of HBM per device.

v0:
```python
import functools
import jax
import jax.numpy as jnp
from jax import lax
from jax.experimental import pallas as pl
from jax.experimental.pallas import tpu as pltpu
from jax.sharding import PartitionSpec as P


HEADS = 40
KV_HEADS = 8
HEAD = 128
EXPERTS = 4
EXTRA = 128
FETCHES = 4


def split3(v):
    parts = []
    for _ in range(3):
        part = v.astype(jnp.bfloat16)
        parts.append(part.astype(jnp.float32))
        v = v - parts[-1]
    return parts


def attend_kernel(len_hbm, ids_hbm, cap_hbm, q_hbm, k_hbm, v_hbm, res_hbm, gain_hbm, router_hbm, sg_hbm,
                  row_ref, stream_ref, sg_out,
                  len_ref, ids_ref, cap_ref, q_ref, k_ref, v_ref, res_ref, gain_ref, router_ref, sem):
    moves = ((q_hbm, q_ref), (k_hbm, k_ref), (len_hbm, len_ref), (v_hbm, v_ref), (res_hbm, res_ref), (gain_hbm, gain_ref),
             (router_hbm, router_ref), (ids_hbm, ids_ref), (cap_hbm, cap_ref), (sg_hbm, sg_out))
    copies = [pltpu.make_async_copy(src, dst, sem.at[i]) for i, (src, dst) in enumerate(moves)]
    for copy in copies:
        copy.start()
    toks, context = k_ref.shape[0], k_ref.shape[1]
    groups = HEADS // KV_HEADS
    width = q_ref.shape[1]
    lane = lax.broadcasted_iota(jnp.int32, (1, EXTRA), 1)
    for copy in copies[:3]:
        copy.wait()
    scores = []
    for r in range(toks):
        queries = q_ref[r:r + 1, :].astype(jnp.float32)
        for h in range(KV_HEADS):
            base = h * groups * HEAD
            heads = [queries[:, base + g * HEAD:base + (g + 1) * HEAD] for g in range(groups)]
            heads += [jnp.zeros((8 - groups, HEAD), jnp.float32)]
            stacked = jnp.concatenate(heads, axis=0).astype(jnp.bfloat16)
            keys = k_ref[r, :, h * HEAD:(h + 1) * HEAD]
            scores.append(lax.dot_general(stacked, keys, (((1,), (1,)), ((), ())), preferred_element_type=jnp.float32))
    key_pos = lax.broadcasted_iota(jnp.int32, (8 * KV_HEADS, context), 1)
    allowed = jnp.concatenate([key_pos < len_ref[r] for r in range(toks)], axis=0)
    scores = jnp.where(allowed, jnp.concatenate(scores, axis=0) * HEAD ** (-0.5), -1e30)
    peak = jnp.max(scores, axis=-1, keepdims=True)
    expo = jnp.where(allowed, jnp.exp(scores - peak), 0.0)
    weights = (expo / jnp.sum(expo, axis=-1, keepdims=True)).astype(jnp.bfloat16).astype(jnp.float32)
    for copy in copies[3:9]:
        copy.wait()
    attended = []
    for r in range(toks):
        for h in range(KV_HEADS):
            top = (r * KV_HEADS + h) * 8
            vals = v_ref[r, :, h * HEAD:(h + 1) * HEAD]
            attended.append(jnp.dot(weights[top:top + 8].astype(jnp.bfloat16), vals, preferred_element_type=jnp.float32))
    attended = [
        jnp.concatenate([attended[r * KV_HEADS + h][g:g + 1] for h in range(KV_HEADS) for g in range(groups)], axis=1)
        for r in range(toks)
    ]
    attended = jnp.concatenate(attended, axis=0).astype(jnp.bfloat16).astype(jnp.float32)
    stream = res_ref[...].astype(jnp.float32) + attended
    mean_square = jnp.mean(stream * stream, axis=-1, keepdims=True)
    normed = (stream * lax.rsqrt(mean_square + 1e-05) * gain_ref[...]).astype(jnp.bfloat16)
    stream_ref[...] = stream
    row_ref[:, :width] = normed
    values = normed.astype(jnp.float32)
    for r in range(toks):
        expert = ids_ref[r]
        column = jnp.zeros((1, width), jnp.float32)
        for e in range(EXPERTS):
            column = jnp.where(expert == e, router_ref[e:e + 1, :].astype(jnp.float32), column)
        logit = jnp.sum(values[r:r + 1] * column, axis=-1, keepdims=True)
        gate = 1.0 / (1.0 + jnp.exp(-logit))
        rank = jnp.int32(0)
        for s in range(r):
            rank = rank + (ids_ref[s] == expert).astype(jnp.int32)
        kept = rank < cap_ref[expert]
        label = jnp.where(kept, expert, -1).astype(jnp.float32)
        one, two, three = split3(gate)
        extra = jnp.where(lane == 0, label, jnp.where(lane == 1, one, jnp.where(lane == 2, two, jnp.where(lane == 3, three, 0.0))))
        row_ref[r:r + 1, width:] = extra.astype(jnp.bfloat16)
    for copy in copies[9:]:
        copy.wait()


def fetch_kernel(start, size, src_hbm, dst_ref, sem):
    source = src_hbm if size is None else src_hbm.at[:, pl.ds(start, size)]
    copy = pltpu.make_async_copy(source, dst_ref, sem)
    copy.start()
    copy.wait()


def ffn_kernel(bn, bd, per_slot, slots, near, front_ref, back_ref, sg_ref, sd_ref, *refs):
    eg_refs, refs = refs[:near], refs[near:]
    su_hbm, eg_hbm, eu_hbm, ed_hbm, keep_ref, send_ref, buf, su_ref, gates, normed, scaled, hidden, shared, sem, su_sem = refs
    width = sg_ref.shape[0]
    units = eu_hbm.shape[1]
    half = keep_ref.shape[0]
    ups = units // bn
    expert_units = units * lax.axis_size(("grp", "sub")) // EXPERTS
    own = (lax.axis_index("grp") * lax.axis_size("sub") + lax.axis_index("sub")) * units // expert_units
    downs = width // (bd * per_slot)

    def columns(src, i):
        return lambda slot: [pltpu.make_async_copy(src.at[:, pl.ds(i * bn, bn)], buf.at[slot, pl.ds(0, width), pl.ds(0, bn)], sem.at[slot, 0])]

    def blocks(i):
        return lambda slot: [
            pltpu.make_async_copy(
                ed_hbm.at[:, pl.ds((i * per_slot + j) * bd, bd)],
                buf.at[slot, pl.ds(j * units, units), pl.ds(0, bd)],
                sem.at[slot, j],
            )
            for j in range(per_slot)
        ]

    loads = []
    for i in range(ups):
        loads += [columns(eg_hbm, i)] if i >= near else []
        loads += [columns(eu_hbm, i)]
    loads += [blocks(i) for i in range(downs)]
    place = iter(range(len(loads)))

    def start(i):
        if i < len(loads):
            for copy in loads[i](i % slots):
                copy.start()

    def arrive():
        i = next(place)
        for copy in loads[i](i % slots):
            copy.wait()
        return i, i % slots

    shared_up = pltpu.make_async_copy(su_hbm, su_ref, su_sem)
    shared_up.start()
    for i in range(slots):
        start(i)

    rows = front_ref.shape[0]
    for part, ref in enumerate((front_ref, back_ref)):
        values = ref[:, :width]
        extra = ref[:, width:].astype(jnp.float32)
        gate = extra[:, 1:2] + extra[:, 2:3] + extra[:, 3:4]
        gate = jnp.where(extra[:, 0:1] == own.astype(jnp.float32), gate, 0.0)
        normed[part * rows:(part + 1) * rows] = values
        scaled[part * rows:(part + 1) * rows] = (values.astype(jnp.float32) * gate).astype(jnp.bfloat16)

    def swish(g, u):
        return (g / (1.0 + jnp.exp(-g)) * u).astype(jnp.bfloat16)

    def times(lhs, rhs):
        return jnp.dot(lhs, rhs, preferred_element_type=jnp.float32)

    g = times(normed[...], sg_ref[...])
    for i in range(near):
        gates[:, i * bn:(i + 1) * bn] = times(scaled[...], eg_refs[i][...])
    shared_up.wait()
    shared[...] = swish(g, times(normed[...], su_ref[...]))
    for i in range(ups):
        if i < near:
            g = gates[:, i * bn:(i + 1) * bn]
        else:
            at, slot = arrive()
            g = times(scaled[...], buf[slot, :width, :bn])
            start(at + slots)
        at, slot = arrive()
        u = times(scaled[...], buf[slot, :width, :bn])
        start(at + slots)
        hidden[:, i * bn:(i + 1) * bn] = swish(g, u)
    for i in range(downs):
        at, slot = arrive()
        for j in range(per_slot):
            col = (i * per_slot + j) * bd
            out = times(shared[...], sd_ref[:, col:col + bd]) + times(hidden[...], buf[slot, j * units:(j + 1) * units, :bd])
            keep_ref[:, col:col + bd] = out[:half]
            send_ref[:, col:col + bd] = out[half:].astype(jnp.bfloat16)
        start(at + slots)


VMEM = pl.BlockSpec(memory_space=pltpu.VMEM)
HBM = pl.BlockSpec(memory_space=pltpu.MemorySpace.HBM)


def nearby(array):
    return pltpu.with_memory_space_constraint(array, pltpu.VMEM)


def afar(array):
    return pltpu.with_memory_space_constraint(array, pltpu.HBM)


def attend_rows(query_rows, cache_keys, cache_values, residual, lengths, ids, capacity, norm_gain, router, shared_gate):
    toks, width = query_rows.shape
    operands = (query_rows, cache_keys, cache_values, residual, norm_gain.reshape(1, width), router.T)
    return pl.pallas_call(
        attend_kernel,
        out_shape=(
            jax.ShapeDtypeStruct((toks, width + EXTRA), jnp.bfloat16),
            jax.ShapeDtypeStruct((toks, width), jnp.float32),
            pltpu.VMEM(shared_gate.shape, shared_gate.dtype),
        ),
        in_specs=[HBM] * 10,
        out_specs=(VMEM,) * 3,
        scratch_shapes=[pltpu.SMEM(a.shape, a.dtype) for a in (lengths, ids, capacity)]
        + [pltpu.VMEM(a.shape, a.dtype) for a in operands]
        + [pltpu.SemaphoreType.DMA((10,))],
        cost_estimate=pl.CostEstimate(flops=0, bytes_accessed=12 << 20, transcendentals=0),
        compiler_params=pltpu.CompilerParams(vmem_limit_bytes=16 << 20),
        name="attend_rows",
    )(*map(afar, (lengths, ids, capacity, *operands, shared_gate)))


def fetch(array, start=0, size=None):
    shape = array.shape if size is None else (array.shape[0], size)
    return pl.pallas_call(
        functools.partial(fetch_kernel, start, size),
        out_shape=pltpu.VMEM(shape, array.dtype),
        in_specs=[HBM],
        out_specs=VMEM,
        scratch_shapes=[pltpu.SemaphoreType.DMA],
        cost_estimate=pl.CostEstimate(flops=0, bytes_accessed=2 * shape[0] * shape[1], transcendentals=0),
        compiler_params=pltpu.CompilerParams(vmem_limit_bytes=1 << 20),
        name="fetch",
    )(afar(array))


def feed_forward(front, back, shared_gate, shared_down, gates, shared_up, expert_gate, expert_up, expert_down, bn):
    count = 2 * front.shape[0]
    width, units = expert_gate.shape
    shared_units = shared_gate.shape[1]
    bd = 512 if width % 512 == 0 else width
    assert units % bn == 0
    per_slot = max(q for q in range(1, width // bd + 1) if (width // bd) % q == 0 and (q == 1 or q * units <= width))
    slot_rows = max(width, per_slot * units)
    slots = 4
    half = count // 2
    weight_bytes = 2 * 3 * width * (units + shared_units)
    return pl.pallas_call(
        functools.partial(ffn_kernel, bn, bd, per_slot, slots, len(gates)),
        out_shape=(pltpu.VMEM((half, width), jnp.float32), pltpu.VMEM((half, width), jnp.bfloat16)),
        in_specs=[VMEM, VMEM] + [VMEM] * (2 + len(gates)) + [HBM] * 4,
        out_specs=(VMEM, VMEM),
        scratch_shapes=[
            pltpu.VMEM((slots, slot_rows, max(bn, bd)), jnp.bfloat16),
            pltpu.VMEM(shared_up.shape, jnp.bfloat16),
            pltpu.VMEM((count, max(1, len(gates)) * bn), jnp.float32),
            pltpu.VMEM((count, width), jnp.bfloat16),
            pltpu.VMEM((count, width), jnp.bfloat16),
            pltpu.VMEM((count, units), jnp.bfloat16),
            pltpu.VMEM((count, shared_units), jnp.bfloat16),
            pltpu.SemaphoreType.DMA((slots, per_slot)),
            pltpu.SemaphoreType.DMA,
        ],
        cost_estimate=pl.CostEstimate(flops=count * weight_bytes, bytes_accessed=weight_bytes, transcendentals=0),
        compiler_params=pltpu.CompilerParams(vmem_limit_bytes=28 << 20),
        name="feed_forward",
    )(front, back, nearby(shared_gate), nearby(shared_down), *map(nearby, gates),
      *map(afar, (shared_up, expert_gate, expert_up, expert_down)))


def per_device(
    steps,
    fetches,
    query_rows,
    cache_keys,
    cache_values,
    residual,
    lengths,
    expert_ids,
    capacity,
    norm_gain,
    router,
    shared_gate,
    shared_up,
    shared_down,
    expert_gate,
    expert_up,
    expert_down,
):
    toks = query_rows.shape[1]
    units = expert_gate.shape[1]
    bn = min(512, units)
    row, stream, near_gate = attend_rows(
        query_rows[0], cache_keys[0], cache_values[0], residual[0], lengths[0],
        expert_ids[0].reshape(toks), capacity, norm_gain, router, shared_gate,
    )
    wanted = [(shared_down,)] + [(expert_gate, i * bn, bn) for i in range(units // bn)]
    near = []
    for i in range(min(fetches, len(wanted))):
        near.append(fetch(*wanted[i]))
    rows = row
    for i, (axis, pairs) in enumerate(steps):
        other = lax.ppermute(rows, axis, pairs)
        if i < len(steps) - 1:
            rows = jnp.concatenate([rows, other], axis=0)
    keep, send = feed_forward(
        rows, other, near_gate, near[0], near[1:],
        shared_up, expert_gate, expert_up, expert_down, bn,
    )
    for i, (axis, pairs) in enumerate(reversed(steps)):
        total = keep + lax.ppermute(send, axis, pairs).astype(jnp.float32)
        half = total.shape[0] // 2
        if i < len(steps) - 1:
            keep, send = total[:half], total[half:].astype(jnp.bfloat16)
    return (stream + total).astype(jnp.bfloat16)[None]


def exchange_steps(mesh):
    steps = []
    for axis in ("grp", "sub"):
        size = mesh.shape[axis]
        assert size & (size - 1) == 0
        bit = size >> 1
        while bit:
            steps.append((axis, tuple((i, i ^ bit) for i in range(size))))
            bit >>= 1
    return tuple(steps)


def solution(mesh):
    placed = (
        P(("grp", "sub"), "rep", None),
        P(("grp", "sub"), "rep", None, None),
        P(("grp", "sub"), "rep", None, None),
        P(("grp", "sub"), "rep", None),
        P(("grp", "sub"), "rep"),
        P(("grp", "sub"), "rep", None),
        P(),
        P(),
        P(),
        P(None, ("grp", "sub")),
        P(None, ("grp", "sub")),
        P(("grp", "sub"), None),
        P(None, ("grp", "sub")),
        P(None, ("grp", "sub")),
        P(("grp", "sub"), None),
    )
    steps = exchange_steps(mesh)
    fetches = min(FETCHES, len(steps))
    return jax.shard_map(
        functools.partial(per_device, steps, fetches),
        mesh=mesh,
        in_specs=placed,
        out_specs=P(("grp", "sub"), "rep", None),
        check_vma=False,
    )
```

profile of v0, /device:TPU:0, one launch (start us, length us, event | category | flops | bytes accessed | tf_op | source)
XLA Modules:
  0.0 63.7 jit_solution(13201425561293711036)
XLA Ops:
  0.0 3.0 %attend_rows.1 = (bf16[2,5248]{1,0:T(2,128)(2,1)S(1)}, f32[2,5120]{1,0:T(2,128)S(1)}, bf16[5120,512]{1,0:T(8,128)(2,1)S(1)}) custom-call(s32[2]{0:T(128)} %bitcast.16, s32[2]{0:T(128)} %bitcast.17, s32[4]{0:T(128)} %cap_hbm.1, bf16[2,5120]{1,0:T(2,128)(2,1)} %bitcast.13, bf16[2,128,1024]{2,1,0:T(8,128)(2,1)} %bitcast.10, bf16[2,128,1024]{2,1,0:T(8,128)(2,1)} %bitcast.11, ...), custom_call_target="tpu_custom_call" | custom-call | bytes 12582912 | tf_op jit(solution)/shard_map/attend_rows/pallas_call | solution.py:205
  3.0 4.1 %collective-permute-start = (bf16[2,5248]{1,0:T(2,128)(2,1)S(1)}, bf16[2,5248]{1,0:T(2,128)(2,1)S(1)}, u32[]{:S(2)}, u32[]{:S(2)}) collective-permute-start(bf16[2,5248]{1,0:T(2,128)(2,1)S(1)} %get-tuple-element.11), channel_id=1, source_target_pairs={{0,8},{2,10},{4,12},{6,14},{8,0},{10,2},{12,4},{14,6},{1,9},{3,11}... | collective-permute-start | bytes 62984 | tf_op jit(solution)/shard_map/ppermute | solution.py:303
  7.1 1.8 %collective-permute-done = bf16[2,5248]{1,0:T(2,128)(2,1)S(1)} collective-permute-done((bf16[2,5248]{1,0:T(2,128)(2,1)S(1)}, bf16[2,5248]{1,0:T(2,128)(2,1)S(1)}, u32[]{:S(2)}, u32[]{:S(2)}) %collective-permute-start) | collective-permute-done | bytes 21024 | tf_op jit(solution)/shard_map/ppermute | solution.py:303
  8.9 2.0 %collective-permute-start.1 = (bf16[4,5248]{1,0:T(4,128)(2,1)S(1)}, bf16[4,5248]{1,0:T(4,128)(2,1)S(1)}, u32[]{:S(2)}, u32[]{:S(2)}) collective-permute-start(bf16[4,5248]{1,0:T(4,128)(2,1)S(1)} %pad_maximum_fusion.2), channel_id=1, source_target_pairs={{0,4},{2,6},{4,0},{6,2},{8,12},{10,14},{12,8},{14,10},{1,5},{3,7},... | collective-permute-start | bytes 125960 | tf_op jit(solution)/shard_map/ppermute | solution.py:303
  10.9 2.1 %collective-permute-done.1 = bf16[4,5248]{1,0:T(4,128)(2,1)S(1)} collective-permute-done((bf16[4,5248]{1,0:T(4,128)(2,1)S(1)}, bf16[4,5248]{1,0:T(4,128)(2,1)S(1)}, u32[]{:S(2)}, u32[]{:S(2)}) %collective-permute-start.1) | collective-permute-done | bytes 42016 | tf_op jit(solution)/shard_map/ppermute | solution.py:303
  13.0 0.1 pad_maximum_fusion.1
  13.1 2.0 %collective-permute-start.2 = (bf16[8,5248]{1,0:T(8,128)(2,1)S(1)}, bf16[8,5248]{1,0:T(8,128)(2,1)S(1)}, u32[]{:S(2)}, u32[]{:S(2)}) collective-permute-start(bf16[8,5248]{1,0:T(8,128)(2,1)S(1)} %pad_maximum_fusion.1), channel_id=1, source_target_pairs={{0,2},{2,0},{4,6},{6,4},{8,10},{10,8},{12,14},{14,12},{1,3},{3,1},... | collective-permute-start | bytes 251912 | tf_op jit(solution)/shard_map/ppermute | solution.py:303
  15.1 2.6 %collective-permute-done.2 = bf16[8,5248]{1,0:T(8,128)(2,1)S(1)} collective-permute-done((bf16[8,5248]{1,0:T(8,128)(2,1)S(1)}, bf16[8,5248]{1,0:T(8,128)(2,1)S(1)}, u32[]{:S(2)}, u32[]{:S(2)}) %collective-permute-start.2) | collective-permute-done | bytes 84000 | tf_op jit(solution)/shard_map/ppermute | solution.py:303
  17.6 0.1 pad_maximum_fusion.front_ref
  17.7 0.1 collective-permute-start.3
  17.8 2.5 %fetch.6.refs_1_ = bf16[5120,512]{1,0:T(8,128)(2,1)S(1)} custom-call(bf16[5120,2048]{1,0:T(8,128)(2,1)} %refs_4_.1), custom_call_target="tpu_custom_call" | custom-call | bytes 5242880 | tf_op jit(solution)/shard_map/fetch/pallas_call | solution.py:225
  20.3 2.5 %fetch.5.refs_0_ = bf16[5120,512]{1,0:T(8,128)(2,1)S(1)} custom-call(bf16[5120,2048]{1,0:T(8,128)(2,1)} %refs_4_.1), custom_call_target="tpu_custom_call" | custom-call | bytes 5242880 | tf_op jit(solution)/shard_map/fetch/pallas_call | solution.py:225
  22.8 2.5 %fetch.7.refs_2_ = bf16[5120,512]{1,0:T(8,128)(2,1)S(1)} custom-call(bf16[5120,2048]{1,0:T(8,128)(2,1)} %refs_4_.1), custom_call_target="tpu_custom_call" | custom-call | bytes 5242880 | tf_op jit(solution)/shard_map/fetch/pallas_call | solution.py:225
  25.3 2.5 %fetch.4.sd_ref = bf16[512,5120]{1,0:T(8,128)(2,1)S(1)} custom-call(bf16[512,5120]{1,0:T(8,128)(2,1)} %src_hbm.4), custom_call_target="tpu_custom_call" | custom-call | bytes 5242880 | tf_op jit(solution)/shard_map/fetch/pallas_call | solution.py:225
  27.8 0.0 collective-permute-done.3.back_ref
  27.9 19.6 %feed_forward.1 = (f32[16,5120]{1,0:T(8,128)S(1)}, bf16[16,5120]{1,0:T(8,128)(2,1)S(1)}) custom-call(bf16[16,5248]{1,0:T(8,128)(2,1)S(1)} %pad_maximum_fusion.front_ref, bf16[16,5248]{1,0:T(8,128)(2,1)S(1)} %collective-permute-done.3.back_ref, bf16[5120,512]{1,0:T(8,128)(2,1)S(1)} %get-tuple-element.12.sg_ref, bf16[512,5120]{1,0:T(8,128)(2,1)S(1)} %fetch.4.sd_ref, ...), custom_call_target="tpu_custom_call" | custom-call | flops 2516582400 | bytes 78643200 | tf_op jit(solution)/shard_map/feed_forward/pallas_call | solution.py:248
  47.5 0.6 collective-permute-start.4
  48.1 1.0 %collective-permute-done.4 = bf16[16,5120]{1,0:T(8,128)(2,1)S(1)} collective-permute-done((bf16[16,5120]{1,0:T(8,128)(2,1)S(1)}, bf16[16,5120]{1,0:T(8,128)(2,1)S(1)}, u32[]{:S(2)}, u32[]{:S(2)}) %collective-permute-start.4) | collective-permute-done | bytes 163872 | tf_op jit(solution)/shard_map/ppermute | solution.py:311
  49.2 2.0 %collective-permute-start.5 = (bf16[8,5120]{1,0:T(8,128)(2,1)S(1)}, bf16[8,5120]{1,0:T(8,128)(2,1)S(1)}, u32[]{:S(2)}, u32[]{:S(2)}) collective-permute-start(bf16[8,5120]{1,0:T(8,128)(2,1)S(1)} %slice.45), channel_id=1, source_target_pairs={{0,2},{2,0},{4,6},{6,4},{8,10},{10,8},{12,14},{14,12},{1,3},{3,1},... | collective-permute-start | bytes 245768 | tf_op jit(solution)/shard_map/ppermute | solution.py:311
  51.1 3.0 %collective-permute-done.5 = bf16[8,5120]{1,0:T(8,128)(2,1)S(1)} collective-permute-done((bf16[8,5120]{1,0:T(8,128)(2,1)S(1)}, bf16[8,5120]{1,0:T(8,128)(2,1)S(1)}, u32[]{:S(2)}, u32[]{:S(2)}) %collective-permute-start.5) | collective-permute-done | bytes 81952 | tf_op jit(solution)/shard_map/ppermute | solution.py:311
  54.2 1.8 %collective-permute-start.6 = (bf16[4,5120]{1,0:T(4,128)(2,1)S(1)}, bf16[4,5120]{1,0:T(4,128)(2,1)S(1)}, u32[]{:S(2)}, u32[]{:S(2)}) collective-permute-start(bf16[4,5120]{1,0:T(4,128)(2,1)S(1)} %slice.46), channel_id=1, source_target_pairs={{0,4},{2,6},{4,0},{6,2},{8,12},{10,14},{12,8},{14,10},{1,5},{3,7},... | collective-permute-start | bytes 122888 | tf_op jit(solution)/shard_map/ppermute | solution.py:311
  55.9 2.3 %collective-permute-done.6 = bf16[4,5120]{1,0:T(4,128)(2,1)S(1)} collective-permute-done((bf16[4,5120]{1,0:T(4,128)(2,1)S(1)}, bf16[4,5120]{1,0:T(4,128)(2,1)S(1)}, u32[]{:S(2)}, u32[]{:S(2)}) %collective-permute-start.6) | collective-permute-done | bytes 40992 | tf_op jit(solution)/shard_map/ppermute | solution.py:311
  58.3 2.8 %collective-permute-start.7 = (bf16[2,5120]{1,0:T(2,128)(2,1)S(1)}, bf16[2,5120]{1,0:T(2,128)(2,1)S(1)}, u32[]{:S(2)}, u32[]{:S(2)}) collective-permute-start(bf16[2,5120]{1,0:T(2,128)(2,1)S(1)} %slice.47), channel_id=1, source_target_pairs={{0,8},{2,10},{4,12},{6,14},{8,0},{10,2},{12,4},{14,6},{1,9},{3,11}... | collective-permute-start | bytes 61448 | tf_op jit(solution)/shard_map/ppermute | solution.py:311
  61.1 1.9 %collective-permute-done.7 = bf16[2,5120]{1,0:T(2,128)(2,1)S(1)} collective-permute-done((bf16[2,5120]{1,0:T(2,128)(2,1)S(1)}, bf16[2,5120]{1,0:T(2,128)(2,1)S(1)}, u32[]{:S(2)}, u32[]{:S(2)}) %collective-permute-start.7) | collective-permute-done | bytes 20512 | tf_op jit(solution)/shard_map/ppermute | solution.py:311
  63.0 0.6 %fusion.2 = bf16[1,2,5120]{2,1,0:T(2,128)(2,1)} fusion(f32[2,5120]{1,0:T(2,128)S(1)} %get-tuple-element.10, bf16[2,5120]{1,0:T(2,128)(2,1)S(1)} %collective-permute-done.7, f32[4,5120]{1,0:T(4,128)S(1)} %slice_add_fusion.1), kind=kLoop, calls=%fused_computation.12 | loop fusion | flops 40960 | bytes 122880 | tf_op jit(solution)/shard_map/broadcast_in_dim | solution.py:315
  (7 shorter events, 0.2 us)
Async XLA Ops:
  3.0 5.9 %collective-permute-start = (bf16[2,5248]{1,0:T(2,128)(2,1)S(1)}, bf16[2,5248]{1,0:T(2,128)(2,1)S(1)}, u32[]{:S(2)}, u32[]{:S(2)}) collective-permute-start(bf16[2,5248]{1,0:T(2,128)(2,1)S(1)} %get-tuple-element.11), channel_id=1, source_target_pairs={{0,8},{2,10},{4,12},{6,14},{8,0},{10,2},{12,4},{14,6},{1,9},{3,11}... | collective-permute-start | bytes 62984 | tf_op jit(solution)/shard_map/ppermute | solution.py:303
  8.9 4.1 %collective-permute-start.1 = (bf16[4,5248]{1,0:T(4,128)(2,1)S(1)}, bf16[4,5248]{1,0:T(4,128)(2,1)S(1)}, u32[]{:S(2)}, u32[]{:S(2)}) collective-permute-start(bf16[4,5248]{1,0:T(4,128)(2,1)S(1)} %pad_maximum_fusion.2), channel_id=1, source_target_pairs={{0,4},{2,6},{4,0},{6,2},{8,12},{10,14},{12,8},{14,10},{1,5},{3,7},... | collective-permute-start | bytes 125960 | tf_op jit(solution)/shard_map/ppermute | solution.py:303
  13.1 4.5 %collective-permute-start.2 = (bf16[8,5248]{1,0:T(8,128)(2,1)S(1)}, bf16[8,5248]{1,0:T(8,128)(2,1)S(1)}, u32[]{:S(2)}, u32[]{:S(2)}) collective-permute-start(bf16[8,5248]{1,0:T(8,128)(2,1)S(1)} %pad_maximum_fusion.1), channel_id=1, source_target_pairs={{0,2},{2,0},{4,6},{6,4},{8,10},{10,8},{12,14},{14,12},{1,3},{3,1},... | collective-permute-start | bytes 251912 | tf_op jit(solution)/shard_map/ppermute | solution.py:303
  17.7 10.1 %collective-permute-start.3 = (bf16[16,5248]{1,0:T(8,128)(2,1)S(1)}, bf16[16,5248]{1,0:T(8,128)(2,1)S(1)}, u32[]{:S(2)}, u32[]{:S(2)}) collective-permute-start(bf16[16,5248]{1,0:T(8,128)(2,1)S(1)} %pad_maximum_fusion.front_ref), channel_id=1, source_target_pairs={{0,1},{1,0},{2,3},{3,2},{4,5},{5,4},{6,7},{7,6},{8,9},{9,8},{10,11... | collective-permute-start | bytes 503816 | tf_op jit(solution)/shard_map/ppermute | solution.py:303
  47.5 1.6 %collective-permute-start.4 = (bf16[16,5120]{1,0:T(8,128)(2,1)S(1)}, bf16[16,5120]{1,0:T(8,128)(2,1)S(1)}, u32[]{:S(2)}, u32[]{:S(2)}) collective-permute-start(bf16[16,5120]{1,0:T(8,128)(2,1)S(1)} %get-tuple-element.14), channel_id=1, source_target_pairs={{0,1},{1,0},{2,3},{3,2},{4,5},{5,4},{6,7},{7,6},{8,9},{9,8},{10,11... | collective-permute-start | bytes 491528 | tf_op jit(solution)/shard_map/ppermute | solution.py:311
  49.2 5.0 %collective-permute-start.5 = (bf16[8,5120]{1,0:T(8,128)(2,1)S(1)}, bf16[8,5120]{1,0:T(8,128)(2,1)S(1)}, u32[]{:S(2)}, u32[]{:S(2)}) collective-permute-start(bf16[8,5120]{1,0:T(8,128)(2,1)S(1)} %slice.45), channel_id=1, source_target_pairs={{0,2},{2,0},{4,6},{6,4},{8,10},{10,8},{12,14},{14,12},{1,3},{3,1},... | collective-permute-start | bytes 245768 | tf_op jit(solution)/shard_map/ppermute | solution.py:311
  54.2 4.1 %collective-permute-start.6 = (bf16[4,5120]{1,0:T(4,128)(2,1)S(1)}, bf16[4,5120]{1,0:T(4,128)(2,1)S(1)}, u32[]{:S(2)}, u32[]{:S(2)}) collective-permute-start(bf16[4,5120]{1,0:T(4,128)(2,1)S(1)} %slice.46), channel_id=1, source_target_pairs={{0,4},{2,6},{4,0},{6,2},{8,12},{10,14},{12,8},{14,10},{1,5},{3,7},... | collective-permute-start | bytes 122888 | tf_op jit(solution)/shard_map/ppermute | solution.py:311
  58.3 4.7 %collective-permute-start.7 = (bf16[2,5120]{1,0:T(2,128)(2,1)S(1)}, bf16[2,5120]{1,0:T(2,128)(2,1)S(1)}, u32[]{:S(2)}, u32[]{:S(2)}) collective-permute-start(bf16[2,5120]{1,0:T(2,128)(2,1)S(1)} %slice.47), channel_id=1, source_target_pairs={{0,8},{2,10},{4,12},{6,14},{8,0},{10,2},{12,4},{14,6},{1,9},{3,11}... | collective-permute-start | bytes 61448 | tf_op jit(solution)/shard_map/ppermute | solution.py:311
where the time goes:
time: 63.9 us; the launch traced here: 63.7 us
  Pallas kernels  32.6 us (51%)
  starting transfers between devices  15.3 us (24%)
  waiting for transfers between devices  14.7 us (23%)
  other arithmetic  0.95 us (1%)
    pallas_call x1, Pallas kernels, feed_forward(): pl.pallas_call(functools.partial(ffn_kernel, bn, bd, per_slot, slots, len...  19.6 us
    pallas_call x4, Pallas kernels, fetch(): pl.pallas_call(functools.partial(fetch_kernel, start, size), out_shape=pl...  9.99 us
    ppermute x4, waiting for transfers between devices, per_device(): total = keep + lax.ppermute(send, axis, pairs).astype(jnp.float32)  8.22 us
    ppermute x4, starting transfers between devices, per_device(): other = lax.ppermute(rows, axis, pairs)  8.14 us
    ppermute x4, starting transfers between devices, per_device(): total = keep + lax.ppermute(send, axis, pairs).astype(jnp.float32)  7.13 us
    ppermute x4, waiting for transfers between devices, per_device(): other = lax.ppermute(rows, axis, pairs)  6.45 us
    pallas_call x1, Pallas kernels, attend_rows(): pl.pallas_call(attend_kernel, out_shape=(jax.ShapeDtypeStruct((toks, widt...  2.97 us
  transfers between devices with their start and end apart: 8, of which 7 were waited for; matrix products, arithmetic and copies ran while one was open for 0% of the time, Pallas kernels for 16%

commit v1 on v0

--- a/solution.py
+++ b/solution.py
@@ -307,11 +307,24 @@
         rows, other, near_gate, near[0], near[1:],
         shared_up, expert_gate, expert_up, expert_down, bn,
     )
-    for i, (axis, pairs) in enumerate(reversed(steps)):
-        total = keep + lax.ppermute(send, axis, pairs).astype(jnp.float32)
-        half = total.shape[0] // 2
-        if i < len(steps) - 1:
-            keep, send = total[:half], total[half:].astype(jnp.bfloat16)
+    back = list(reversed(steps))
+    i = 0
+    while i < len(back):
+        if i and i + 1 < len(back):
+            (axis, first), (_, second) = back[i], back[i + 1]
+            both = tuple((src, second[dst][1]) for src, dst in first)
+            size = keep.shape[0]
+            total = keep
+            for part, pairs in enumerate((second, first, both)):
+                piece = send[part * size:(part + 1) * size]
+                total = total + lax.ppermute(piece, axis, pairs).astype(jnp.float32)
+            i += 2
+        else:
+            total = keep + lax.ppermute(send, *back[i]).astype(jnp.float32)
+            i += 1
+        rows_left = total.shape[0]
+        share = rows_left // 4 if i + 1 < len(back) else rows_left // 2
+        keep, send = total[:share], total[share:].astype(jnp.bfloat16)
     return (stream + total).astype(jnp.bfloat16)[None]
 
 

time: 63.9 us -> 62.4 us (0.977)
  waiting for transfers between devices: 14.7 us -> 13.5 us
    ppermute x4 -> x5, waiting for transfers between devices: 8.22 us -> 7.04 us  [the longest x3 3.89 us: per_device(): total = total + lax.ppermute(piece, axis, pairs).astype(jnp.float32)]
    ppermute x4 -> x5, starting transfers between devices: 7.13 us -> 6.73 us  [the longest x3 3.55 us: per_device(): total = total + lax.ppermute(piece, axis, pairs).astype(jnp.float32)]
  transfers between devices with their start and end apart: 8 -> 9, of which waited for: 7 -> 8; matrix products, arithmetic and copies ran while one was open for 0% -> 0% of each run, Pallas kernels for 16% -> 16%
where the time goes in v1:
time: 62.4 us; the launch traced here: 62.1 us
  Pallas kernels  32.6 us (52%)
  starting transfers between devices  14.9 us (24%)
  waiting for transfers between devices  13.5 us (22%)
  other arithmetic  0.96 us (2%)
    pallas_call x1, Pallas kernels, feed_forward(): pl.pallas_call(functools.partial(ffn_kernel, bn, bd, per_slot, slots, len...  19.6 us
    pallas_call x4, Pallas kernels, fetch(): pl.pallas_call(functools.partial(fetch_kernel, start, size), out_shape=pl...  9.99 us
    ppermute x4, starting transfers between devices, per_device(): other = lax.ppermute(rows, axis, pairs)  8.14 us
    ppermute x4, waiting for transfers between devices, per_device(): other = lax.ppermute(rows, axis, pairs)  6.45 us
    ppermute x3, waiting for transfers between devices, per_device(): total = total + lax.ppermute(piece, axis, pairs).astype(jnp.float32)  3.89 us
    ppermute x3, starting transfers between devices, per_device(): total = total + lax.ppermute(piece, axis, pairs).astype(jnp.float32)  3.55 us
    ppermute x2, starting transfers between devices, per_device(): total = keep + lax.ppermute(send, *back[i]).astype(jnp.float32)  3.18 us
    ppermute x2, waiting for transfers between devices, per_device(): total = keep + lax.ppermute(send, *back[i]).astype(jnp.float32)  3.15 us
  transfers between devices with their start and end apart: 9, of which 8 were waited for; matrix products, arithmetic and copies ran while one was open for 0% of the time, Pallas kernels for 16%

profile of v1, /device:TPU:0, one launch (start us, length us, event | category | flops | bytes accessed | tf_op | source)
XLA Modules:
  0.0 62.1 jit_solution(18028677145108076254)
XLA Ops:
  0.0 3.0 %attend_rows.1 = (bf16[2,5248]{1,0:T(2,128)(2,1)S(1)}, f32[2,5120]{1,0:T(2,128)S(1)}, bf16[5120,512]{1,0:T(8,128)(2,1)S(1)}) custom-call(s32[2]{0:T(128)} %bitcast.16, s32[2]{0:T(128)} %bitcast.17, s32[4]{0:T(128)} %cap_hbm.1, bf16[2,5120]{1,0:T(2,128)(2,1)} %bitcast.13, bf16[2,128,1024]{2,1,0:T(8,128)(2,1)} %bitcast.10, bf16[2,128,1024]{2,1,0:T(8,128)(2,1)} %bitcast.11, ...), custom_call_target="tpu_custom_call" | custom-call | bytes 12582912 | tf_op jit(solution)/shard_map/attend_rows/pallas_call | solution.py:205
  3.0 4.1 %collective-permute-start = (bf16[2,5248]{1,0:T(2,128)(2,1)S(1)}, bf16[2,5248]{1,0:T(2,128)(2,1)S(1)}, u32[]{:S(2)}, u32[]{:S(2)}) collective-permute-start(bf16[2,5248]{1,0:T(2,128)(2,1)S(1)} %get-tuple-element.11), channel_id=1, source_target_pairs={{0,8},{2,10},{4,12},{6,14},{8,0},{10,2},{12,4},{14,6},{1,9},{3,11}... | collective-permute-start | bytes 62984 | tf_op jit(solution)/shard_map/ppermute | solution.py:303
  7.1 1.8 %collective-permute-done = bf16[2,5248]{1,0:T(2,128)(2,1)S(1)} collective-permute-done((bf16[2,5248]{1,0:T(2,128)(2,1)S(1)}, bf16[2,5248]{1,0:T(2,128)(2,1)S(1)}, u32[]{:S(2)}, u32[]{:S(2)}) %collective-permute-start) | collective-permute-done | bytes 21024 | tf_op jit(solution)/shard_map/ppermute | solution.py:303
  8.9 2.0 %collective-permute-start.1 = (bf16[4,5248]{1,0:T(4,128)(2,1)S(1)}, bf16[4,5248]{1,0:T(4,128)(2,1)S(1)}, u32[]{:S(2)}, u32[]{:S(2)}) collective-permute-start(bf16[4,5248]{1,0:T(4,128)(2,1)S(1)} %pad_maximum_fusion.2), channel_id=1, source_target_pairs={{0,4},{2,6},{4,0},{6,2},{8,12},{10,14},{12,8},{14,10},{1,5},{3,7},... | collective-permute-start | bytes 125960 | tf_op jit(solution)/shard_map/ppermute | solution.py:303
  10.9 2.1 %collective-permute-done.1 = bf16[4,5248]{1,0:T(4,128)(2,1)S(1)} collective-permute-done((bf16[4,5248]{1,0:T(4,128)(2,1)S(1)}, bf16[4,5248]{1,0:T(4,128)(2,1)S(1)}, u32[]{:S(2)}, u32[]{:S(2)}) %collective-permute-start.1) | collective-permute-done | bytes 42016 | tf_op jit(solution)/shard_map/ppermute | solution.py:303
  13.0 0.1 pad_maximum_fusion.1
  13.1 2.0 %collective-permute-start.2 = (bf16[8,5248]{1,0:T(8,128)(2,1)S(1)}, bf16[8,5248]{1,0:T(8,128)(2,1)S(1)}, u32[]{:S(2)}, u32[]{:S(2)}) collective-permute-start(bf16[8,5248]{1,0:T(8,128)(2,1)S(1)} %pad_maximum_fusion.1), channel_id=1, source_target_pairs={{0,2},{2,0},{4,6},{6,4},{8,10},{10,8},{12,14},{14,12},{1,3},{3,1},... | collective-permute-start | bytes 251912 | tf_op jit(solution)/shard_map/ppermute | solution.py:303
  15.1 2.6 %collective-permute-done.2 = bf16[8,5248]{1,0:T(8,128)(2,1)S(1)} collective-permute-done((bf16[8,5248]{1,0:T(8,128)(2,1)S(1)}, bf16[8,5248]{1,0:T(8,128)(2,1)S(1)}, u32[]{:S(2)}, u32[]{:S(2)}) %collective-permute-start.2) | collective-permute-done | bytes 84000 | tf_op jit(solution)/shard_map/ppermute | solution.py:303
  17.6 0.1 pad_maximum_fusion.front_ref
  17.7 0.1 collective-permute-start.3
  17.8 2.5 %fetch.6.refs_1_ = bf16[5120,512]{1,0:T(8,128)(2,1)S(1)} custom-call(bf16[5120,2048]{1,0:T(8,128)(2,1)} %refs_4_.1), custom_call_target="tpu_custom_call" | custom-call | bytes 5242880 | tf_op jit(solution)/shard_map/fetch/pallas_call | solution.py:225
  20.3 2.5 %fetch.5.refs_0_ = bf16[5120,512]{1,0:T(8,128)(2,1)S(1)} custom-call(bf16[5120,2048]{1,0:T(8,128)(2,1)} %refs_4_.1), custom_call_target="tpu_custom_call" | custom-call | bytes 5242880 | tf_op jit(solution)/shard_map/fetch/pallas_call | solution.py:225
  22.8 2.5 %fetch.7.refs_2_ = bf16[5120,512]{1,0:T(8,128)(2,1)S(1)} custom-call(bf16[5120,2048]{1,0:T(8,128)(2,1)} %refs_4_.1), custom_call_target="tpu_custom_call" | custom-call | bytes 5242880 | tf_op jit(solution)/shard_map/fetch/pallas_call | solution.py:225
  25.3 2.5 %fetch.4.sd_ref = bf16[512,5120]{1,0:T(8,128)(2,1)S(1)} custom-call(bf16[512,5120]{1,0:T(8,128)(2,1)} %src_hbm.4), custom_call_target="tpu_custom_call" | custom-call | bytes 5242880 | tf_op jit(solution)/shard_map/fetch/pallas_call | solution.py:225
  27.8 0.0 collective-permute-done.3.back_ref
  27.9 19.6 %feed_forward.1 = (f32[16,5120]{1,0:T(8,128)S(1)}, bf16[16,5120]{1,0:T(8,128)(2,1)S(1)}) custom-call(bf16[16,5248]{1,0:T(8,128)(2,1)S(1)} %pad_maximum_fusion.front_ref, bf16[16,5248]{1,0:T(8,128)(2,1)S(1)} %collective-permute-done.3.back_ref, bf16[5120,512]{1,0:T(8,128)(2,1)S(1)} %get-tuple-element.12.sg_ref, bf16[512,5120]{1,0:T(8,128)(2,1)S(1)} %fetch.4.sd_ref, ...), custom_call_target="tpu_custom_call" | custom-call | flops 2516582400 | bytes 78643200 | tf_op jit(solution)/shard_map/feed_forward/pallas_call | solution.py:248
  47.5 0.6 collective-permute-start.4
  48.1 1.0 %collective-permute-done.4 = bf16[16,5120]{1,0:T(8,128)(2,1)S(1)} collective-permute-done((bf16[16,5120]{1,0:T(8,128)(2,1)S(1)}, bf16[16,5120]{1,0:T(8,128)(2,1)S(1)}, u32[]{:S(2)}, u32[]{:S(2)}) %collective-permute-start.4) | collective-permute-done | bytes 163872 | tf_op jit(solution)/shard_map/ppermute | solution.py:323
  49.1 0.1 fusion.6
  49.2 2.0 %collective-permute-start.5 = (bf16[4,5120]{1,0:T(4,128)(2,1)S(1)}, bf16[4,5120]{1,0:T(4,128)(2,1)S(1)}, u32[]{:S(2)}, u32[]{:S(2)}) collective-permute-start(bf16[4,5120]{1,0:T(4,128)(2,1)S(1)} %get-tuple-element.17), channel_id=1, source_target_pairs={{0,4},{2,6},{4,0},{6,2},{8,12},{10,14},{12,8},{14,10},{1,5},{3,7},... | collective-permute-start | bytes 122888 | tf_op jit(solution)/shard_map/ppermute | solution.py:320
  51.2 1.5 %collective-permute-start.7 = (bf16[4,5120]{1,0:T(4,128)(2,1)S(1)}, bf16[4,5120]{1,0:T(4,128)(2,1)S(1)}, u32[]{:S(2)}, u32[]{:S(2)}) collective-permute-start(bf16[4,5120]{1,0:T(4,128)(2,1)S(1)} %get-tuple-element.18), channel_id=1, source_target_pairs={{0,6},{2,4},{4,2},{6,0},{8,14},{10,12},{12,10},{14,8},{1,7},{3,5},... | collective-permute-start | bytes 122888 | tf_op jit(solution)/shard_map/ppermute | solution.py:320
  52.6 0.1 collective-permute-start.6
  52.8 0.5 collective-permute-done.5
  53.3 2.8 %collective-permute-done.7 = bf16[4,5120]{1,0:T(4,128)(2,1)S(1)} collective-permute-done((bf16[4,5120]{1,0:T(4,128)(2,1)S(1)}, bf16[4,5120]{1,0:T(4,128)(2,1)S(1)}, u32[]{:S(2)}, u32[]{:S(2)}) %collective-permute-start.7) | collective-permute-done | bytes 40992 | tf_op jit(solution)/shard_map/ppermute | solution.py:320
  56.1 0.6 collective-permute-done.6
  56.7 2.6 %collective-permute-start.8 = (bf16[2,5120]{1,0:T(2,128)(2,1)S(1)}, bf16[2,5120]{1,0:T(2,128)(2,1)S(1)}, u32[]{:S(2)}, u32[]{:S(2)}) collective-permute-start(bf16[2,5120]{1,0:T(2,128)(2,1)S(1)} %slice.49), channel_id=1, source_target_pairs={{0,8},{2,10},{4,12},{6,14},{8,0},{10,2},{12,4},{14,6},{1,9},{3,11}... | collective-permute-start | bytes 61448 | tf_op jit(solution)/shard_map/ppermute | solution.py:323
  59.3 2.1 %collective-permute-done.8 = bf16[2,5120]{1,0:T(2,128)(2,1)S(1)} collective-permute-done((bf16[2,5120]{1,0:T(2,128)(2,1)S(1)}, bf16[2,5120]{1,0:T(2,128)(2,1)S(1)}, u32[]{:S(2)}, u32[]{:S(2)}) %collective-permute-start.8) | collective-permute-done | bytes 20512 | tf_op jit(solution)/shard_map/ppermute | solution.py:323
  61.5 0.6 %fusion.4 = bf16[1,2,5120]{2,1,0:T(2,128)(2,1)} fusion(f32[2,5120]{1,0:T(2,128)S(1)} %get-tuple-element.10, bf16[2,5120]{1,0:T(2,128)(2,1)S(1)} %collective-permute-done.8, f32[4,5120]{1,0:T(4,128)S(1)} %fusion.1), kind=kLoop, calls=%fused_computation.11 | loop fusion | flops 40960 | bytes 122880 | tf_op jit(solution)/shard_map/broadcast_in_dim | solution.py:328
  (4 shorter events, 0.2 us)
Async XLA Ops:
  3.0 5.9 %collective-permute-start = (bf16[2,5248]{1,0:T(2,128)(2,1)S(1)}, bf16[2,5248]{1,0:T(2,128)(2,1)S(1)}, u32[]{:S(2)}, u32[]{:S(2)}) collective-permute-start(bf16[2,5248]{1,0:T(2,128)(2,1)S(1)} %get-tuple-element.11), channel_id=1, source_target_pairs={{0,8},{2,10},{4,12},{6,14},{8,0},{10,2},{12,4},{14,6},{1,9},{3,11}... | collective-permute-start | bytes 62984 | tf_op jit(solution)/shard_map/ppermute | solution.py:303
  8.9 4.1 %collective-permute-start.1 = (bf16[4,5248]{1,0:T(4,128)(2,1)S(1)}, bf16[4,5248]{1,0:T(4,128)(2,1)S(1)}, u32[]{:S(2)}, u32[]{:S(2)}) collective-permute-start(bf16[4,5248]{1,0:T(4,128)(2,1)S(1)} %pad_maximum_fusion.2), channel_id=1, source_target_pairs={{0,4},{2,6},{4,0},{6,2},{8,12},{10,14},{12,8},{14,10},{1,5},{3,7},... | collective-permute-start | bytes 125960 | tf_op jit(solution)/shard_map/ppermute | solution.py:303
  13.1 4.5 %collective-permute-start.2 = (bf16[8,5248]{1,0:T(8,128)(2,1)S(1)}, bf16[8,5248]{1,0:T(8,128)(2,1)S(1)}, u32[]{:S(2)}, u32[]{:S(2)}) collective-permute-start(bf16[8,5248]{1,0:T(8,128)(2,1)S(1)} %pad_maximum_fusion.1), channel_id=1, source_target_pairs={{0,2},{2,0},{4,6},{6,4},{8,10},{10,8},{12,14},{14,12},{1,3},{3,1},... | collective-permute-start | bytes 251912 | tf_op jit(solution)/shard_map/ppermute | solution.py:303
  17.7 10.1 %collective-permute-start.3 = (bf16[16,5248]{1,0:T(8,128)(2,1)S(1)}, bf16[16,5248]{1,0:T(8,128)(2,1)S(1)}, u32[]{:S(2)}, u32[]{:S(2)}) collective-permute-start(bf16[16,5248]{1,0:T(8,128)(2,1)S(1)} %pad_maximum_fusion.front_ref), channel_id=1, source_target_pairs={{0,1},{1,0},{2,3},{3,2},{4,5},{5,4},{6,7},{7,6},{8,9},{9,8},{10,11... | collective-permute-start | bytes 503816 | tf_op jit(solution)/shard_map/ppermute | solution.py:303
  47.5 1.6 %collective-permute-start.4 = (bf16[16,5120]{1,0:T(8,128)(2,1)S(1)}, bf16[16,5120]{1,0:T(8,128)(2,1)S(1)}, u32[]{:S(2)}, u32[]{:S(2)}) collective-permute-start(bf16[16,5120]{1,0:T(8,128)(2,1)S(1)} %get-tuple-element.14), channel_id=1, source_target_pairs={{0,1},{1,0},{2,3},{3,2},{4,5},{5,4},{6,7},{7,6},{8,9},{9,8},{10,11... | collective-permute-start | bytes 491528 | tf_op jit(solution)/shard_map/ppermute | solution.py:323
  49.2 4.1 %collective-permute-start.5 = (bf16[4,5120]{1,0:T(4,128)(2,1)S(1)}, bf16[4,5120]{1,0:T(4,128)(2,1)S(1)}, u32[]{:S(2)}, u32[]{:S(2)}) collective-permute-start(bf16[4,5120]{1,0:T(4,128)(2,1)S(1)} %get-tuple-element.17), channel_id=1, source_target_pairs={{0,4},{2,6},{4,0},{6,2},{8,12},{10,14},{12,8},{14,10},{1,5},{3,7},... | collective-permute-start | bytes 122888 | tf_op jit(solution)/shard_map/ppermute | solution.py:320
  51.2 4.9 %collective-permute-start.7 = (bf16[4,5120]{1,0:T(4,128)(2,1)S(1)}, bf16[4,5120]{1,0:T(4,128)(2,1)S(1)}, u32[]{:S(2)}, u32[]{:S(2)}) collective-permute-start(bf16[4,5120]{1,0:T(4,128)(2,1)S(1)} %get-tuple-element.18), channel_id=1, source_target_pairs={{0,6},{2,4},{4,2},{6,0},{8,14},{10,12},{12,10},{14,8},{1,7},{3,5},... | collective-permute-start | bytes 122888 | tf_op jit(solution)/shard_map/ppermute | solution.py:320
  52.6 4.0 %collective-permute-start.6 = (bf16[4,5120]{1,0:T(4,128)(2,1)S(1)}, bf16[4,5120]{1,0:T(4,128)(2,1)S(1)}, u32[]{:S(2)}, u32[]{:S(2)}) collective-permute-start(bf16[4,5120]{1,0:T(4,128)(2,1)S(1)} %get-tuple-element.19), channel_id=1, source_target_pairs={{0,2},{2,0},{4,6},{6,4},{8,10},{10,8},{12,14},{14,12},{1,3},{3,1},... | collective-permute-start | bytes 122888 | tf_op jit(solution)/shard_map/ppermute | solution.py:320
  56.7 4.7 %collective-permute-start.8 = (bf16[2,5120]{1,0:T(2,128)(2,1)S(1)}, bf16[2,5120]{1,0:T(2,128)(2,1)S(1)}, u32[]{:S(2)}, u32[]{:S(2)}) collective-permute-start(bf16[2,5120]{1,0:T(2,128)(2,1)S(1)} %slice.49), channel_id=1, source_target_pairs={{0,8},{2,10},{4,12},{6,14},{8,0},{10,2},{12,4},{14,6},{1,9},{3,11}... | collective-permute-start | bytes 61448 | tf_op jit(solution)/shard_map/ppermute | solution.py:323
